TPU v7x, 128 devices: a whole 4x4x4 slice. The times are simulated.
128 devices in a mesh: inst: 8 (over z_lo, x), space: 16 (over z_hi, y, core).
Axes of the slice: x: 4, y: 4, z: 4 (z_hi: 2, z_lo: 2; z = z_hi * 2 + z_lo), core: 2. Of those that a mesh axis runs over, the one named last changes fastest.
Arguments:
- field_start: float32 [32, 256, 64, 128], P('inst', 'space'), may hold values from -6 to 6
- source: float32 [32, 256, 64, 128], P('inst', 'space'), may hold values from -6 to 6
- material: int32 [256, 64, 128], P('space'), may hold values from 0 to 7
- face_flags: int32 [32, 3, 256, 64, 128], P('inst', None, 'space'), may hold values from 0 to 1
- disp_table: float32 [8], replicated, may hold values from 0.3 to 3
- perm_table: float32 [8], replicated, may hold values from 0.2 to 2
Outputs:
- residual: float32 [32, 256, 64, 128], P('inst', 'space')
- field: float32 [32, 256, 64, 128], P('inst', 'space')
All inputs are finite; a program needn't handle non-finite values.
Results may differ from a plain program's by a relative error of at most 0.00005.
Values sent between devices are 32-bit elements; how exact they have to be, the bound alone decides.
A program may use at most 128 MiB of HBM per device.

v0:
```python
import jax
import jax.numpy as jnp
from jax import lax
from jax.sharding import PartitionSpec as P

NT = 32
omega_scale = 0.25
decay_rate = 0.3
relax_weight = 0.8


def shifted(shard, axis, by):
    count = lax.axis_size(axis)
    pairs = [(i, i + by) for i in range(count) if 0 <= i + by < count]
    return lax.ppermute(shard, axis, pairs)


def with_halo(block, sides, width):
    for axis, dim in sides:
        count = lax.axis_size(axis)
        forward = [(i, i + 1) for i in range(count - 1)]
        backward = [(target, source) for source, target in forward]
        low = lax.ppermute(
            lax.slice_in_dim(block, block.shape[dim] - width, None, axis=dim), axis, forward
        )
        high = lax.ppermute(lax.slice_in_dim(block, 0, width, axis=dim), axis, backward)
        block = jnp.concatenate([low, block, high], axis=dim)
    return block


def spectral_matrix(first, count):
    rows = first + jnp.arange(count)
    cols = jnp.arange(NT)
    diff = rows[:, None] - cols[None, :]
    angle = jnp.pi * diff.astype(jnp.float32) / NT
    parity = 1.0 - 2.0 * (diff % 2).astype(jnp.float32)
    safe = jnp.where(diff == 0, 1.0, jnp.sin(angle))
    return jnp.where(diff == 0, 0.0, 0.5 * parity * jnp.cos(angle) / safe)


def lookup(material, table):
    total = jnp.zeros(material.shape, jnp.float32)
    for klass in range(table.shape[0]):
        total = total + jnp.where(material == klass, table[klass], 0.0)
    return total


def next_along(field, axis):
    count = field.shape[axis]
    zeros = jnp.zeros_like(lax.slice_in_dim(field, 0, 1, axis=axis))
    return jnp.concatenate([lax.slice_in_dim(field, 1, count, axis=axis), zeros], axis)


def prev_along(field, axis):
    count = field.shape[axis]
    zeros = jnp.zeros_like(lax.slice_in_dim(field, 0, 1, axis=axis))
    return jnp.concatenate([zeros, lax.slice_in_dim(field, 0, count - 1, axis=axis)], axis)


def face_terms(field, up_val, lo_val, kappa, lo_kappa, flow, lo_flow):
    return (
        kappa * (field - up_val)
        + lo_kappa * (field - lo_val)
        + jnp.maximum(flow, 0.0) * field
        + jnp.minimum(flow, 0.0) * up_val
        - jnp.maximum(lo_flow, 0.0) * lo_val
        - jnp.minimum(lo_flow, 0.0) * field
    )


def diag_terms(kappa, lo_kappa, flow, lo_flow):
    return kappa + lo_kappa + jnp.maximum(flow, 0.0) - jnp.minimum(lo_flow, 0.0)


def body(field_start, source, material, face_flags, disp_table, perm_table):
    count = field_start.shape[0]
    first = lax.axis_index("inst") * count
    kappa = lookup(material, disp_table)
    speed = lookup(material, perm_table)
    moments = (first + jnp.arange(count)).astype(jnp.float32)
    tide = 1.0 + 0.5 * jnp.cos(2.0 * jnp.pi * moments / NT)
    velocity = (
        speed[None, None]
        * tide[:, None, None, None, None]
        * (1.0 - 2.0 * face_flags.astype(jnp.float32))
    )
    top_plane = jnp.concatenate([kappa[-1:], velocity[:, 0, -1]], 0)
    below = shifted(top_plane, "space", 1)
    low_kappa_z = jnp.concatenate([below[:1], kappa[:-1]], 0)
    low_flow_z = jnp.concatenate([below[1:, None], velocity[:, 0, :-1]], 1)
    kappa_wide = kappa[None]
    diag = decay_rate + jnp.zeros_like(field_start)
    diag = diag + diag_terms(kappa_wide, low_kappa_z[None], velocity[:, 0], low_flow_z)
    for axis in (1, 2):
        flow = velocity[:, axis]
        diag = diag + diag_terms(
            kappa_wide, prev_along(kappa, axis)[None], flow, prev_along(flow, axis + 1)
        )
    dmat_rows = spectral_matrix(first, count)

    def coupled(field):
        piece = lax.all_gather(field, "inst", axis=0, tiled=True)
        flat = piece.reshape(piece.shape[0], -1)
        product = jnp.dot(
            dmat_rows, flat, precision=lax.Precision.HIGHEST, preferred_element_type=jnp.float32
        )
        return product.reshape(jnp.zeros(field.shape, jnp.float32).shape)

    def residual_of(field):
        padded = with_halo(field, (("space", 1),), 1)
        total = decay_rate * field
        total = total + face_terms(
            field,
            padded[:, 2:],
            padded[:, :-2],
            kappa_wide,
            low_kappa_z[None],
            velocity[:, 0],
            low_flow_z,
        )
        for axis in (1, 2):
            flow = velocity[:, axis]
            total = total + face_terms(
                field,
                next_along(field, axis + 1),
                prev_along(field, axis + 1),
                kappa_wide,
                prev_along(kappa, axis)[None],
                flow,
                prev_along(flow, axis + 1),
            )
        return omega_scale * coupled(field) + total - source

    residual = residual_of(field_start)
    middle = field_start - relax_weight * residual / diag
    second = residual_of(middle)
    field = middle - relax_weight * second / diag
    return (residual, field)


def solution(mesh):
    return jax.shard_map(
        body,
        mesh=mesh,
        in_specs=(
            P("inst", "space", None, None),
            P("inst", "space", None, None),
            P("space", None, None),
            P("inst", None, "space", None, None),
            P(),
            P(),
        ),
        out_specs=(P("inst", "space", None, None), P("inst", "space", None, None)),
        check_vma=False,
    )
```

profile of v0, /device:TPU:1, one launch (start us, length us, event | category | flops | bytes accessed | tf_op | source)
XLA Modules:
  0.0 476.9 jit_solution(4694018413515174211)
XLA Ops:
  9.5 3.3 collective-permute-start
  12.8 3.2 collective-permute-start.2
  16.7 7.8 %select_add_fusion.1 = (f32[16,64,128]{2,1,0:T(8,128)S(1)}, pred[16,64,128]{2,1,0:T(8,128)(4,1)S(1)}, pred[16,64,128]{2,1,0:T(8,128)(4,1)S(1)}, pred[16,64,128]{...) fusion(f32[]{:T(128)} %bitcast.10, f32[]{:T(128)} %bitcast.9, ...), kind=kLoop, calls=%fused_computation.68 | loop fusion | flops 3014656 | bytes 2097184 | tf_op jit(solution)/shard_map/add | solution.py:44
  25.8 6.5 %select_add_fusion = f32[16,64,128]{2,1,0:T(8,128)S(1)} fusion(pred[16,64,128]{2,1,0:T(8,128)(4,1)} %get-tuple-element.18, pred[16,64,128]{2,1,0:T(8,128)(4,1)S(1)} %get-tuple-element.17, pred[16,64,128]{2,1,0:T(8,128)(4,1)S(1)} %get-tuple-element.16, pred[16,64,128]{2,1,0:T(8,128)(4,1)S(1)} %get-tuple-element.15, ...), kind=kLoop, calls=%fused_computation.67 | loop fusion | flops 1966080 | bytes 1572896 | tf_op jit(solution)/shard_map/add | solution.py:44
  32.6 4.0 fusion.6
  36.7 2.3 collective-permute-start.1
  39.0 2.4 slice_bitcast_fusion.1
  41.4 2.4 fusion.81
  43.9 2.9 fusion.82
  48.3 1.9 pad_maximum_fusion.5
  50.1 135.6 %all-gather.3.cloned.1.call-done = f32[32,16,64,128]{3,2,1,0:T(8,128)} async-done(((f32[4,16,64,128]{3,2,1,0:T(8,128)}), f32[32,16,64,128]{3,2,1,0:T(8,128)}) %all-gather.3.cloned.1.call-update) | async-done | bytes 16777232 | tf_op jit(solution)/shard_map/all_gather | solution.py:102
  185.7 15.2 %copy.176 = f32[4,8,1024,128]{3,1,2,0:T(8,128)S(1)} copy(f32[4,8,1024,128]{3,2,1,0:T(8,128)} %bitcast.116) | data formatting | bytes 33554432
  200.9 6.9 %copy.152 = f32[4,8,1024,128]{3,2,1,0:T(8,128)} copy(f32[4,8,1024,128]{3,1,2,0:T(8,128)S(1)} %copy.176) | data formatting | bytes 33554432
  207.8 25.3 %fusion.2 = f32[4,16,64,128]{3,0,2,1:T(4,128)} fusion(f32[16,64,128,32]{2,1,0,3:T(8,128)} %bitcast.109, s32[4]{0:T(128)S(1)} %iota_add_fusion), kind=kOutput, calls=%fused_computation.4 | convolution fusion | flops 201329536 | bytes 18874384 | tf_op jit(solution)/shard_map/dot_general | solution.py:104
  233.2 11.2 %divide_subtract_fusion = (f32[4,16,64,128]{3,2,1,0:T(8,128)}, f32[4,16,64,128]{3,2,1,0:T(8,128)}) fusion(f32[4,16,64,128]{3,2,1,0:T(8,128)S(1)} %copy-done.2, f32[4,16,64,127]{3,2,1,0:T(8,128)S(1)} %bitcast.114, f32[4,16,63,128]{3,2,1,0:T(8,128)S(1)} %bitcast.112, f32[4,3,16,64,128]{4,3,2,0,1:T(8,128)S(1)} %bitcast.105, ...), kind=kLoop, calls=%fused_computation.61 | loop fusion | flops 38273024 | bytes 35241984 | tf_op jit(solution)/shard_map/sub | solution.py:135
  246.7 2.6 collective-permute-start.3
  249.3 2.9 collective-permute-start.4
  252.2 2.4 fusion.77
  254.7 2.9 fusion.78
  257.6 155.4 %all-gather.5.cloned.1.call-done = f32[32,16,64,128]{3,2,1,0:T(8,128)} async-done(((f32[4,16,64,128]{3,2,1,0:T(8,128)}), f32[32,16,64,128]{3,2,1,0:T(8,128)}) %all-gather.5.cloned.1.call-update) | async-done | bytes 16777232 | tf_op jit(solution)/shard_map/all_gather | solution.py:102
  413.0 15.2 %copy.175 = f32[4,8,1024,128]{3,1,2,0:T(8,128)S(1)} copy(f32[4,8,1024,128]{3,2,1,0:T(8,128)} %bitcast.117) | data formatting | bytes 33554432
  428.2 6.9 %copy.154 = f32[4,8,1024,128]{3,2,1,0:T(8,128)} copy(f32[4,8,1024,128]{3,1,2,0:T(8,128)S(1)} %copy.175) | data formatting | bytes 33554432
  435.1 24.9 %fusion = f32[4,16,64,128]{3,0,2,1:T(4,128)} fusion(f32[16,64,128,32]{2,1,0,3:T(8,128)} %bitcast.108, s32[4]{0:T(128)S(1)} %iota_add_fusion), kind=kOutput, calls=%fused_computation.2 | convolution fusion | flops 201329536 | bytes 18874384 | tf_op jit(solution)/shard_map/dot_general | solution.py:104
  460.1 9.8 %fusion.18 = f32[4,16,64,128]{3,2,1,0:T(8,128)} fusion(f32[4,16,64,128]{3,2,1,0:T(8,128)S(1)} %copy-done, f32[4,16,64,128]{3,2,1,0:T(8,128)} %param.7, f32[4,1,64,128]{3,2,1,0:T(8,128)S(1)} %collective-permute-done.4, f32[4,1,64,128]{3,2,1,0:T(8,128)S(1)} %collective-permute-done.3, f32[4,16,64,128]{3,0,2,1:T(4,128)} %fusion, ...), kind=kLoop, calls=%fused_computation.22 | loop fusion | flops 38273024 | bytes 33144832 | tf_op jit(solution)/shard_map/sub | solution.py:137
  (57 shorter events, 8.4 us)
Async XLA Ops:
  7.2 1.6 copy-start.2
  7.2 8.8 %copy-start.10 = (f32[8]{0:T(128)S(1)}, f32[8]{0:T(128)}, u32[]{:S(2)}) copy-start(f32[8]{0:T(128)} %param.10) | copy-start | bytes 100
  7.2 17.9 %copy-start.11 = (f32[8]{0:T(128)S(1)}, f32[8]{0:T(128)}, u32[]{:S(2)}) copy-start(f32[8]{0:T(128)} %param.11) | copy-start | bytes 100
  7.2 178.5 %all-gather.3.cloned.1.call-start = ((), (), s32[]{:S(2)}) async-start(), calls=%async_computation | async-start | bytes 18874368 | tf_op jit(solution)/shard_map/all_gather | solution.py:102
  7.9 405.1 %all-gather.5.cloned.1.call-start = ((), (), s32[]{:S(2)}) async-start(), calls=%async_computation.1 | async-start | bytes 18874368 | tf_op jit(solution)/shard_map/all_gather | solution.py:102
  9.5 223.7 %collective-permute-start = (f32[4,1,64,128]{3,2,1,0:T(8,128)}, f32[4,1,64,128]{3,2,1,0:T(8,128)}, u32[]{:S(2)}, u32[]{:S(2)}) collective-permute-start(f32[4,1,64,128]{3,2,1,0:T(8,128)} %get-tuple-element.27), channel_id=1, source_target_pairs={{1,0},{2,1},{3,2},{4,3},{5,4},{6,5},{7,6},{8,7},{9,8},{10,9},{11,1... | collective-permute-start | bytes 393224 | tf_op jit(solution)/shard_map/ppermute | solution.py:26
  12.8 220.3 %collective-permute-start.2 = (f32[4,1,64,128]{3,2,1,0:T(8,128)}, f32[4,1,64,128]{3,2,1,0:T(8,128)}, u32[]{:S(2)}, u32[]{:S(2)}) collective-permute-start(f32[4,1,64,128]{3,2,1,0:T(8,128)} %get-tuple-element.28), channel_id=1, source_target_pairs={{0,1},{1,2},{2,3},{3,4},{4,5},{5,6},{6,7},{7,8},{8,9},{9,10},{10,1... | collective-permute-start | bytes 393224 | tf_op jit(solution)/shard_map/ppermute | solution.py:23
  32.6 4.1 copy-start.9
  36.6 10.2 %copy-start.1 = (f32[4,3,16,64,128]{4,3,2,0,1:T(8,128)}, f32[4,3,16,64,128]{4,3,2,0,1:T(8,128)S(1)}, u32[]{:S(2)}) copy-start(f32[4,3,16,64,128]{4,3,2,0,1:T(8,128)S(1)} %fusion.6) | copy-start | bytes 18874372
  36.7 11.5 %collective-permute-start.1 = (f32[5,64,128]{2,1,0:T(8,128)S(1)}, f32[5,64,128]{2,1,0:T(8,128)S(1)}, u32[]{:S(2)}, u32[]{:S(2)}) collective-permute-start(f32[5,64,128]{2,1,0:T(8,128)S(1)} %pad_maximum_fusion.6), channel_id=1, source_target_pairs={{0,1},{1,2},{2,3},{3,4},{4,5},{5,6},{6,7},{7,8},{8,9},{9,10},{10,1... | collective-permute-start | bytes 491528 | tf_op jit(solution)/shard_map/ppermute | solution.py:15
  207.8 25.3 %slice-start = ((s8[6291456]{0:T(1024)(128)(4,1)}), s8[4194304]{0:T(1024)(128)(4,1)S(1)}, s32[]{:S(2)}) async-start(s8[6291456]{0:T(1024)(128)(4,1)} %bitcast.104), calls=%async_computation.2 | async-start | bytes 8388608
  207.8 25.3 %slice-start.1 = ((s8[6291456]{0:T(1024)(128)(4,1)}), s8[2097152]{0:T(1024)(128)(4,1)S(1)}, s32[]{:S(2)}) async-start(s8[6291456]{0:T(1024)(128)(4,1)} %bitcast.104), calls=%async_computation.3 | async-start | bytes 4194304
  207.8 25.3 %copy-start.3 = (f32[4,16,64,128]{3,2,1,0:T(8,128)S(1)}, f32[4,16,64,128]{3,2,1,0:T(8,128)}, u32[]{:S(2)}) copy-start(f32[4,16,64,128]{3,2,1,0:T(8,128)} %get-tuple-element.19) | copy-start | bytes 6291460
  207.8 25.3 %copy-start.5 = (f32[4,16,64,128]{3,2,1,0:T(8,128)S(1)}, f32[4,16,64,128]{3,2,1,0:T(8,128)}, u32[]{:S(2)}) copy-start(f32[4,16,64,128]{3,2,1,0:T(8,128)} %get-tuple-element.20) | copy-start | bytes 6291460
  207.8 25.3 %copy-start.8 = (f32[16,64,128]{2,1,0:T(8,128)S(1)}, f32[16,64,128]{2,1,0:T(8,128)}, u32[]{:S(2)}) copy-start(f32[16,64,128]{2,1,0:T(8,128)} %get-tuple-element.34) | copy-start | bytes 1572868
  244.4 1.6 copy-start
  246.7 213.3 %collective-permute-start.3 = (f32[4,1,64,128]{3,2,1,0:T(8,128)}, f32[4,1,64,128]{3,2,1,0:T(8,128)S(1)}, u32[]{:S(2)}, u32[]{:S(2)}) collective-permute-start(f32[4,1,64,128]{3,2,1,0:T(8,128)} %get-tuple-element.25), channel_id=1, source_target_pairs={{1,0},{2,1},{3,2},{4,3},{5,4},{6,5},{7,6},{8,7},{9,8},{10,9},{11,1... | collective-permute-start | bytes 393224 | tf_op jit(solution)/shard_map/ppermute | solution.py:26
  249.3 210.7 %collective-permute-start.4 = (f32[4,1,64,128]{3,2,1,0:T(8,128)}, f32[4,1,64,128]{3,2,1,0:T(8,128)S(1)}, u32[]{:S(2)}, u32[]{:S(2)}) collective-permute-start(f32[4,1,64,128]{3,2,1,0:T(8,128)} %get-tuple-element.26), channel_id=1, source_target_pairs={{0,1},{1,2},{2,3},{3,4},{4,5},{5,6},{6,7},{7,8},{8,9},{9,10},{10,1... | collective-permute-start | bytes 393224 | tf_op jit(solution)/shard_map/ppermute | solution.py:23
  435.1 24.9 %slice-start.2 = ((s8[6291456]{0:T(1024)(128)(4,1)}), s8[4194304]{0:T(1024)(128)(4,1)S(1)}, s32[]{:S(2)}) async-start(s8[6291456]{0:T(1024)(128)(4,1)} %bitcast.106), calls=%async_computation.4 | async-start | bytes 8388608
  435.1 24.9 %slice-start.3 = ((s8[6291456]{0:T(1024)(128)(4,1)}), s8[2097152]{0:T(1024)(128)(4,1)S(1)}, s32[]{:S(2)}) async-start(s8[6291456]{0:T(1024)(128)(4,1)} %bitcast.106), calls=%async_computation.5 | async-start | bytes 4194304
  435.1 25.0 %copy-start.4 = (f32[4,16,64,128]{3,2,1,0:T(8,128)S(1)}, f32[4,16,64,128]{3,2,1,0:T(8,128)}, u32[]{:S(2)}) copy-start(f32[4,16,64,128]{3,2,1,0:T(8,128)} %get-tuple-element.19) | copy-start | bytes 6291460
  435.1 25.0 %copy-start.6 = (f32[4,16,64,128]{3,2,1,0:T(8,128)S(1)}, f32[4,16,64,128]{3,2,1,0:T(8,128)}, u32[]{:S(2)}) copy-start(f32[4,16,64,128]{3,2,1,0:T(8,128)} %get-tuple-element.20) | copy-start | bytes 6291460
  435.1 25.0 %copy-start.7 = (f32[4,15,64,128]{3,2,1,0:T(8,128)S(1)}, f32[4,15,64,128]{3,2,1,0:T(8,128)}, u32[]{:S(2)}) copy-start(f32[4,15,64,128]{3,2,1,0:T(8,128)} %slice_bitcast_fusion.2) | copy-start | bytes 5898244
Sparse Core Ops, SparseCore 0:
  9.7 176.0 all-gather.2
  244.5 168.3 all-gather.4
where the time goes:
time: 484 us; the launch traced here: 477 us
  waiting for transfers between devices  292 us (60%)
  local copies, waits for them, and re-layouts  64.5 us (13%)
  matrix products  50.2 us (10%)
  other arithmetic  41.5 us (9%)
  between operations  14.6 us (3%)
  starting transfers between devices  14.4 us (3%)
    all_gather x2, waiting for transfers between devices, coupled(): piece = lax.all_gather(field, 'inst', axis=0, tiled=True)  291 us
    dot_general x2, matrix products, coupled(): jnp.dot(dmat_rows, flat, precision=lax.Precision.HIGHEST, preferred_eleme...  50.2 us
    unnamed x36, local copies, waits for them, and re-layouts  46.5 us
    add x2, other arithmetic, lookup(): total = total + jnp.where(material == klass, table[klass], 0.0)  14.2 us
    sub x1, other arithmetic, body(): middle = field_start - relax_weight * residual / diag  11.2 us
    slice x4, local copies, waits for them, and re-layouts, next_along(): lax.slice_in_dim(field, 1, count, axis=axis)  10.7 us
    sub x1, other arithmetic, body(): field = middle - relax_weight * second / diag  9.77 us
  transfers between devices with their start and end apart: 7, of which 2 were waited for; matrix products, arithmetic and copies ran while one was open for 28% of the time, Pallas kernels for 0%

commit v1 on v0

--- a/solution.py
+++ b/solution.py
@@ -99,7 +99,9 @@
     dmat_rows = spectral_matrix(first, count)
 
     def coupled(field):
-        piece = lax.all_gather(field, "inst", axis=0, tiled=True)
+        piece = jnp.concatenate(
+            lax.all_to_all(jnp.stack([field] * lax.axis_size("inst")), "inst", 0, 0), axis=0
+        )
         flat = piece.reshape(piece.shape[0], -1)
         product = jnp.dot(
             dmat_rows, flat, precision=lax.Precision.HIGHEST, preferred_element_type=jnp.float32

time: 484 us -> 659 us (1.36)
  the two profiles are of different devices: /device:TPU:1 before, /device:TPU:6 now
where the time goes in v1:
time: 659 us; the launch traced here: 652 us
  waiting for transfers between devices  453 us (69%)
  local copies, waits for them, and re-layouts  85.7 us (13%)
  matrix products  50.2 us (8%)
  other arithmetic  37.7 us (6%)
  starting transfers between devices  24.2 us (4%)
    all_to_all x2, waiting for transfers between devices, coupled(): lax.all_to_all(jnp.stack([field] * lax.axis_size('inst')), 'inst', 0, 0)  453 us
    dot_general x2, matrix products, coupled(): jnp.dot(dmat_rows, flat, precision=lax.Precision.HIGHEST, preferred_eleme...  50.2 us
    unnamed x32, local copies, waits for them, and re-layouts  28.2 us
    another operation x2, local copies, waits for them, and re-layouts, coupled(): flat = piece.reshape(piece.shape[0], -1)  24.2 us
    another operation x2, local copies, waits for them, and re-layouts, coupled(): jnp.stack([field] * lax.axis_size('inst'))  17.4 us
  transfers between devices with their start and end apart: 7, of which 2 were waited for; matrix products, arithmetic and copies ran while one was open for 21% of the time, Pallas kernels for 0%

profile of v1, /device:TPU:6, one launch (start us, length us, event | category | flops | bytes accessed | tf_op | source)
XLA Modules:
  0.0 652.1 jit_solution(3142719800188936686)
XLA Ops:
  0.6 9.5 %stack.4 = f32[8,4,16,64,128]{4,3,2,1,0:T(8,128)} broadcast(f32[4,16,64,128]{3,2,1,0:T(8,128)} %param.6), dimensions={1,2,3,4} | broadcast | bytes 18874368 | tf_op jit(solution)/shard_map/stack | solution.py:103
  10.1 6.3 all-to-all-start
  17.0 5.6 select_add_fusion.1
  23.3 5.3 select_add_fusion
  28.9 4.0 fusion.6
  35.8 4.7 collective-permute-start.2
  40.5 2.4 slice_bitcast_fusion.1
  42.9 2.3 fusion.81
  45.2 2.7 fusion.82
  51.4 215.1 %all-to-all-done = f32[8,4,16,64,128]{4,3,2,1,0:T(8,128)} async-done(((f32[8,4,16,64,128]{4,3,2,1,0:T(8,128)}), f32[8,4,16,64,128]{4,3,2,1,0:T(8,128)}, u32[]{:S(2)}, u32[]{:S(2)}) %all-to-all-start) | async-done | bytes 16777248 | tf_op jit(solution)/shard_map/all_to_all | solution.py:103
  266.4 12.1 %reshape_reshape.6 = f32[32,131072]{1,0:T(8,128)} reshape(f32[8,4,16,64,128]{4,3,2,1,0:T(8,128)} %all-to-all-done) | data formatting | bytes 33554432 | tf_op jit(solution)/shard_map/reshape;reshape | solution.py:105
  278.5 14.1 %copy.106 = f32[4,8,1024,128]{3,2,1,0:T(8,128)} copy(f32[4,8,1024,128]{3,1,2,0:T(8,128)} %bitcast.99) | data formatting | bytes 33554432
  292.6 25.3 %fusion.2 = f32[4,16,64,128]{3,0,2,1:T(4,128)} fusion(f32[16,64,128,32]{2,1,0,3:T(8,128)} %bitcast.100, s32[4]{0:T(128)S(1)} %iota_add_fusion), kind=kOutput, calls=%fused_computation.2 | convolution fusion | flops 201329536 | bytes 18874384 | tf_op jit(solution)/shard_map/dot_general | solution.py:106
  318.0 10.7 %divide_subtract_fusion = (f32[4,16,64,128]{3,2,1,0:T(8,128)S(1)}, f32[4,16,64,128]{3,2,1,0:T(8,128)}) fusion(f32[4,16,64,128]{3,2,1,0:T(8,128)S(1)} %copy-done.2, f32[4,16,64,127]{3,2,1,0:T(8,128)} %bitcast.106, f32[4,16,63,128]{3,2,1,0:T(8,128)S(1)} %bitcast.104, f32[4,3,16,64,128]{4,3,2,0,1:T(8,128)S(1)} %bitcast.95, ...), kind=kLoop, calls=%fused_computation.59 | loop fusion | flops 38273024 | bytes 35241984 | tf_op jit(solution)/shard_map/sub | solution.py:137
  328.6 7.9 %stack.5 = f32[8,4,16,64,128]{4,3,2,1,0:T(8,128)} broadcast(f32[4,16,64,128]{3,2,1,0:T(8,128)S(1)} %get-tuple-element.6), dimensions={1,2,3,4} | broadcast | bytes 18874368 | tf_op jit(solution)/shard_map/stack | solution.py:103
  336.5 6.2 all-to-all-start.1
  344.7 3.0 collective-permute-start.4
  347.8 2.3 fusion.77
  350.1 2.7 fusion.78
  352.8 238.1 %all-to-all-done.1 = f32[8,4,16,64,128]{4,3,2,1,0:T(8,128)} async-done(((f32[8,4,16,64,128]{4,3,2,1,0:T(8,128)}), f32[8,4,16,64,128]{4,3,2,1,0:T(8,128)}, u32[]{:S(2)}, u32[]{:S(2)}) %all-to-all-start.1) | async-done | bytes 16777248 | tf_op jit(solution)/shard_map/all_to_all | solution.py:103
  591.0 12.1 %reshape_reshape.7 = f32[32,131072]{1,0:T(8,128)} reshape(f32[8,4,16,64,128]{4,3,2,1,0:T(8,128)} %all-to-all-done.1) | data formatting | bytes 33554432 | tf_op jit(solution)/shard_map/reshape;reshape | solution.py:105
  603.1 14.1 %copy.107 = f32[4,8,1024,128]{3,2,1,0:T(8,128)} copy(f32[4,8,1024,128]{3,1,2,0:T(8,128)} %bitcast.101) | data formatting | bytes 33554432
  617.2 24.9 %fusion = f32[4,16,64,128]{3,0,2,1:T(4,128)} fusion(f32[16,64,128,32]{2,1,0,3:T(8,128)} %bitcast.98, s32[4]{0:T(128)S(1)} %iota_add_fusion), kind=kOutput, calls=%fused_computation | convolution fusion | flops 201329536 | bytes 18874384 | tf_op jit(solution)/shard_map/dot_general | solution.py:106
  642.1 9.8 %fusion.18 = f32[4,16,64,128]{3,2,1,0:T(8,128)} fusion(f32[4,16,64,128]{3,2,1,0:T(8,128)S(1)} %get-tuple-element.6, f32[4,16,64,128]{3,2,1,0:T(8,128)} %param.7, f32[4,1,64,128]{3,2,1,0:T(8,128)S(1)} %collective-permute-done.4, f32[4,1,64,128]{3,2,1,0:T(8,128)S(1)} %collective-permute-done.3, f32[4,16,64,128]{3,0,2,1:T(4,128)} %fusion, ...), kind=kLoop, calls=%fused_computation.20 | loop fusion | flops 38273024 | bytes 33144832 | tf_op jit(solution)/shard_map/sub | solution.py:139
  (55 shorter events, 9.7 us)
Async XLA Ops:
  10.1 6.3 copy-start.9
  10.1 6.9 %copy-start.8 = (s32[16,64,128]{2,1,0:T(8,128)S(1)}, s32[16,64,128]{2,1,0:T(8,128)}, u32[]{:S(2)}) copy-start(s32[16,64,128]{2,1,0:T(8,128)} %param.8) | copy-start | bytes 1572868
  10.1 256.3 %all-to-all-start = ((f32[8,4,16,64,128]{4,3,2,1,0:T(8,128)}), f32[8,4,16,64,128]{4,3,2,1,0:T(8,128)}, u32[]{:S(2)}, u32[]{:S(2)}) async-start(f32[8,4,16,64,128]{4,3,2,1,0:T(8,128)} %stack.4), calls=%async_computation | async-start | bytes 33554432 | tf_op jit(solution)/shard_map/all_to_all | solution.py:103
  16.4 6.3 copy-start.10
  28.9 5.5 copy-start.1
  33.0 15.0 %copy-start = (f32[4,3,16,64,128]{4,3,2,0,1:T(8,128)}, f32[4,3,16,64,128]{4,3,2,0,1:T(8,128)S(1)}, u32[]{:S(2)}) copy-start(f32[4,3,16,64,128]{4,3,2,0,1:T(8,128)S(1)} %fusion.6) | copy-start | bytes 18874372
  33.0 16.4 %collective-permute-start.1 = (f32[5,64,128]{2,1,0:T(8,128)S(1)}, f32[5,64,128]{2,1,0:T(8,128)S(1)}, u32[]{:S(2)}, u32[]{:S(2)}) collective-permute-start(f32[5,64,128]{2,1,0:T(8,128)S(1)} %pad_maximum_fusion.6), channel_id=1, source_target_pairs={{0,1},{1,2},{2,3},{3,4},{4,5},{5,6},{6,7},{7,8},{8,9},{9,10},{10,1... | collective-permute-start | bytes 491528 | tf_op jit(solution)/shard_map/ppermute | solution.py:15
  34.5 283.4 %collective-permute-start = (f32[4,1,64,128]{3,2,1,0:T(8,128)S(1)}, f32[4,1,64,128]{3,2,1,0:T(8,128)S(1)}, u32[]{:S(2)}, u32[]{:S(2)}) collective-permute-start(f32[4,1,64,128]{3,2,1,0:T(8,128)S(1)} %get-tuple-element.25), channel_id=1, source_target_pairs={{1,0},{2,1},{3,2},{4,3},{5,4},{6,5},{7,6},{8,7},{9,8},{10,9},{11,1... | collective-permute-start | bytes 393224 | tf_op jit(solution)/shard_map/ppermute | solution.py:26
  35.8 282.1 %collective-permute-start.2 = (f32[4,1,64,128]{3,2,1,0:T(8,128)S(1)}, f32[4,1,64,128]{3,2,1,0:T(8,128)S(1)}, u32[]{:S(2)}, u32[]{:S(2)}) collective-permute-start(f32[4,1,64,128]{3,2,1,0:T(8,128)S(1)} %get-tuple-element.26), channel_id=1, source_target_pairs={{0,1},{1,2},{2,3},{3,4},{4,5},{5,6},{6,7},{7,8},{8,9},{9,10},{10,1... | collective-permute-start | bytes 393224 | tf_op jit(solution)/shard_map/ppermute | solution.py:23
  292.6 25.3 %slice-start = ((s8[6291456]{0:T(1024)(128)(4,1)}), s8[4194304]{0:T(1024)(128)(4,1)S(1)}, s32[]{:S(2)}) async-start(s8[6291456]{0:T(1024)(128)(4,1)} %bitcast.94), calls=%async_computation.2 | async-start | bytes 8388608
  292.6 25.3 %slice-start.1 = ((s8[6291456]{0:T(1024)(128)(4,1)}), s8[2097152]{0:T(1024)(128)(4,1)S(1)}, s32[]{:S(2)}) async-start(s8[6291456]{0:T(1024)(128)(4,1)} %bitcast.94), calls=%async_computation.3 | async-start | bytes 4194304
  292.6 25.3 %copy-start.2 = (f32[4,16,64,128]{3,2,1,0:T(8,128)S(1)}, f32[4,16,64,128]{3,2,1,0:T(8,128)}, u32[]{:S(2)}) copy-start(f32[4,16,64,128]{3,2,1,0:T(8,128)} %param.6) | copy-start | bytes 6291460
  292.6 25.3 %copy-start.3 = (f32[4,16,64,128]{3,2,1,0:T(8,128)S(1)}, f32[4,16,64,128]{3,2,1,0:T(8,128)}, u32[]{:S(2)}) copy-start(f32[4,16,64,128]{3,2,1,0:T(8,128)} %get-tuple-element.17) | copy-start | bytes 6291460
  292.6 25.3 %copy-start.7 = (f32[16,64,128]{2,1,0:T(8,128)S(1)}, f32[16,64,128]{2,1,0:T(8,128)}, u32[]{:S(2)}) copy-start(f32[16,64,128]{2,1,0:T(8,128)} %get-tuple-element.32) | copy-start | bytes 1572868
  336.5 254.5 %all-to-all-start.1 = ((f32[8,4,16,64,128]{4,3,2,1,0:T(8,128)}), f32[8,4,16,64,128]{4,3,2,1,0:T(8,128)}, u32[]{:S(2)}, u32[]{:S(2)}) async-start(f32[8,4,16,64,128]{4,3,2,1,0:T(8,128)} %stack.5), calls=%async_computation.1 | async-start | bytes 33554432 | tf_op jit(solution)/shard_map/all_to_all | solution.py:103
  343.4 298.6 %collective-permute-start.3 = (f32[4,1,64,128]{3,2,1,0:T(8,128)}, f32[4,1,64,128]{3,2,1,0:T(8,128)S(1)}, u32[]{:S(2)}, u32[]{:S(2)}) collective-permute-start(f32[4,1,64,128]{3,2,1,0:T(8,128)} %get-tuple-element.23), channel_id=1, source_target_pairs={{1,0},{2,1},{3,2},{4,3},{5,4},{6,5},{7,6},{8,7},{9,8},{10,9},{11,1... | collective-permute-start | bytes 393224 | tf_op jit(solution)/shard_map/ppermute | solution.py:26
  344.7 297.4 %collective-permute-start.4 = (f32[4,1,64,128]{3,2,1,0:T(8,128)}, f32[4,1,64,128]{3,2,1,0:T(8,128)S(1)}, u32[]{:S(2)}, u32[]{:S(2)}) collective-permute-start(f32[4,1,64,128]{3,2,1,0:T(8,128)} %get-tuple-element.24), channel_id=1, source_target_pairs={{0,1},{1,2},{2,3},{3,4},{4,5},{5,6},{6,7},{7,8},{8,9},{9,10},{10,1... | collective-permute-start | bytes 393224 | tf_op jit(solution)/shard_map/ppermute | solution.py:23
  617.1 24.9 %slice-start.2 = ((s8[6291456]{0:T(1024)(128)(4,1)}), s8[4194304]{0:T(1024)(128)(4,1)S(1)}, s32[]{:S(2)}) async-start(s8[6291456]{0:T(1024)(128)(4,1)} %bitcast.96), calls=%async_computation.4 | async-start | bytes 8388608
  617.1 25.0 %slice-start.3 = ((s8[6291456]{0:T(1024)(128)(4,1)}), s8[2097152]{0:T(1024)(128)(4,1)S(1)}, s32[]{:S(2)}) async-start(s8[6291456]{0:T(1024)(128)(4,1)} %bitcast.96), calls=%async_computation.5 | async-start | bytes 4194304
  617.1 25.0 %copy-start.4 = (f32[4,16,64,128]{3,2,1,0:T(8,128)S(1)}, f32[4,16,64,128]{3,2,1,0:T(8,128)}, u32[]{:S(2)}) copy-start(f32[4,16,64,128]{3,2,1,0:T(8,128)} %get-tuple-element.17) | copy-start | bytes 6291460
  617.1 25.0 %copy-start.5 = (f32[4,16,64,128]{3,2,1,0:T(8,128)S(1)}, f32[4,16,64,128]{3,2,1,0:T(8,128)}, u32[]{:S(2)}) copy-start(f32[4,16,64,128]{3,2,1,0:T(8,128)} %get-tuple-element.18) | copy-start | bytes 6291460
  617.1 25.0 %copy-start.6 = (f32[4,15,64,128]{3,2,1,0:T(8,128)S(1)}, f32[4,15,64,128]{3,2,1,0:T(8,128)}, u32[]{:S(2)}) copy-start(f32[4,15,64,128]{3,2,1,0:T(8,128)} %slice_bitcast_fusion.2) | copy-start | bytes 5898244
